TPU v7x, 32 devices: a whole 2x2x4 slice. The times are simulated.
32 devices in a mesh: dom: 32 (over z, y, x, core).
Axes of the slice: x: 2, y: 2, z: 4, core: 2. Of those that a mesh axis runs over, the one named last changes fastest.
Arguments:
- modal_dofs: float32 [35, 9, 8192], P(None, None, 'dom'), may hold values from -6 to 6
- jacobian: float32 [3, 8192], P(None, 'dom'), may hold values from 0.2 to 0.8
- face_area: float32 [4, 8192], P(None, 'dom'), may hold values from 0.1 to 0.4
- cluster_id: int32 [8192], P('dom'), may hold values from 0 to 1
- target_slot: int32 [8192], P('dom'), may hold values from 0 to 383, as said below
- ghost_slots: int32 [32, 8, 6], P('dom'), may hold values from 0 to 383
- face_neighbours: int32 [4, 12288], P(None, 'dom'), may hold values from 0 to 431, as said below
- stiffness: float32 [3, 35, 35], replicated, may hold values from -1 to 1
- star_matrix: float32 [3, 9, 9], replicated, may hold values from -2 to 2
- face_minus: float32 [4, 35, 35], replicated, may hold values from -1 to 1
- face_plus: float32 [4, 35, 35], replicated, may hold values from -1 to 1
- solver_minus: float32 [4, 9, 9], replicated, may hold values from -2 to 2
- solver_plus: float32 [4, 9, 9], replicated, may hold values from -2 to 2
Outputs:
- updated: float32 [35, 9, 8192], P(None, None, 'dom')
Inputs may be any that keep to these rules, and one draw needn't show every extreme that they name: `target_slot`: within the 256 elements of one block the values are distinct. One owner, the same for every block, receives 12 elements from every block. `face_neighbours`: values from 384 on address the ghost table of 48 entries.
All inputs are finite; a program needn't handle non-finite values.
Results may differ from a plain program's by a relative error of at most 0.0003.
Values sent between devices are 32-bit elements; how exact they have to be, the bound alone decides.
A program may use at most 64 MiB of HBM per device.

v0:
```python
import functools
import math

import jax
import jax.numpy as jnp
import numpy as np
from jax import lax
from jax.experimental import pallas as pl
from jax.experimental.pallas import tpu as pltpu
from jax.sharding import PartitionSpec as P

ORDER = 5
LANES = 128
SUB = 8
MESH = pl.DeviceIdType.MESH
neighbour_steps = (1, -1, 2, -2, 3, -3, 4, -4)


def coefficients(lower_end, upper_end):
    return [
        (upper_end ** (degree + 1) - lower_end ** (degree + 1)) / math.factorial(degree + 1)
        for degree in range(ORDER)
    ]


def round_up(value, multiple):
    return -(-value // multiple) * multiple


def dot(a, b, dims=((1,), (0,))):
    return lax.dot_general(a, b, (dims, ((), ())), preferred_element_type=jnp.float32)


def halves(x):
    hi = x.astype(jnp.bfloat16)
    lo = (x - hi.astype(jnp.float32)).astype(jnp.bfloat16)
    return hi, lo


def thirds(x):
    hi = x.astype(jnp.bfloat16)
    rest = x - hi.astype(jnp.float32)
    mid = rest.astype(jnp.bfloat16)
    lo = (rest - mid.astype(jnp.float32)).astype(jnp.bfloat16)
    return hi, mid, lo


def triple(x):
    hi, lo = halves(x)
    return jnp.concatenate([hi, lo, hi], axis=1)


def as_bf16(mask):
    return mask.astype(jnp.float32).astype(jnp.bfloat16)


def kernel(
    n,
    extra_at,
    dofs_ref,
    jac_ref,
    area_ref,
    cluster_ref,
    target_ref,
    ghost_ref,
    face_ref,
    spread_mode_ref,
    spread_quant_ref,
    stiff_ref,
    star_ref,
    face_minus_ref,
    face_plus_ref,
    solver_minus_ref,
    solver_plus_ref,
    out_ref,
    staged,
    send_a,
    recv_a,
    send_b,
    recv_b,
    ghost_send,
    ghost_recv,
    state,
    later_ref,
    w_derive,
    w_local,
    w_plus,
    pick_face,
    pick_ghost,
    pick_back,
    ghost_idx,
    face_idx,
    target_idx,
    send_sem,
    recv_sem,
    back_send_sem,
    back_recv_sem,
    ghost_send_sem,
    ghost_recv_sem,
):
    me = lax.axis_index("dom")
    flat, elements = dofs_ref.shape
    width = staged.shape[0]
    slots = state.shape[0]
    cap = slots // n
    beside = len(neighbour_steps)
    ghosts = ghost_ref.shape[1]
    faces = face_ref.shape[0]
    dirs = stiff_ref.shape[0]

    barrier = pltpu.get_barrier_semaphore()

    def greet(d, carry):
        pl.semaphore_signal(barrier, inc=1, device_id=(lax.rem(me + d, n),), device_id_type=MESH)
        return carry

    lax.fori_loop(1, n, greet, 0)

    staged[...] = jnp.zeros_like(staged)
    staged[0:flat, :] = dofs_ref[...]
    staged[extra_at : extra_at + dirs, :] = jac_ref[...]
    staged[extra_at + dirs : extra_at + dirs + faces, :] = area_ref[...]
    staged[extra_at + dirs + faces : extra_at + dirs + faces + 1, :] = 1.0 + cluster_ref[
        ...
    ].astype(jnp.float32)
    scatter = as_bf16(
        lax.broadcasted_iota(jnp.int32, (slots, elements), 0) == target_ref[...]
    )
    hi, mid, lo = thirds(staged[...])
    nt = ((1,), (1,))
    rows = (dot(scatter, lo, nt) + dot(scatter, mid, nt)) + dot(scatter, hi, nt)
    for r in range(n):
        send_a[r] = rows[r * cap : (r + 1) * cap, :]

    pl.semaphore_wait(barrier, n - 1)

    def piece(source, landing, out_sem, in_sem, d):
        peer = lax.rem(me + d, n)
        return pltpu.make_async_remote_copy(
            src_ref=source.at[peer],
            dst_ref=landing.at[me],
            send_sem=out_sem.at[d],
            recv_sem=in_sem.at[d],
            device_id=(peer,),
            device_id_type=MESH,
        )

    def start_all(source, landing, out_sem, in_sem):
        def body(d, carry):
            piece(source, landing, out_sem, in_sem, d).start()
            return carry

        lax.fori_loop(1, n, body, 0)
        landing[me] = source[me]

    def wait_all(source, landing, out_sem, in_sem):
        def body(d, carry):
            piece(source, landing, out_sem, in_sem, d).wait()
            return carry

        lax.fori_loop(1, n, body, 0)

    start_all(send_a, recv_a, send_sem, recv_sem)

    target_idx[...] = jnp.zeros_like(target_idx)
    target_idx[0:1, :] = target_ref[...].astype(jnp.float32)
    target_col = jnp.transpose(target_idx[...])[:, 0:1].astype(jnp.int32)
    pick_back[...] = as_bf16(
        lax.broadcasted_iota(jnp.int32, (elements, slots), 1) == target_col
    )
    ghost_idx[...] = jnp.full_like(ghost_idx, -1.0)
    ghost_idx[:, 0:ghosts] = ghost_ref[...].astype(jnp.float32)
    ghost_cols = jnp.transpose(ghost_idx[...])[0:SUB, :].astype(jnp.int32)
    place = lax.broadcasted_iota(jnp.int32, (SUB, slots), 1)
    for b in range(beside):
        pick_ghost[b] = (place == ghost_cols[:, b : b + 1]).astype(jnp.float32)
    face_idx[...] = jnp.zeros_like(face_idx)
    listed = face_ref[...]
    shift = jnp.zeros_like(listed)
    for b in range(1, beside):
        shift = shift + (listed >= slots + b * ghosts).astype(jnp.int32) * (SUB - ghosts)
    face_idx[0:faces, :] = (listed + shift).astype(jnp.float32)
    face_cols = jnp.transpose(face_idx[...]).astype(jnp.int32)
    reach = pick_face.shape[2]
    for f in range(faces):
        pick_face[f] = as_bf16(
            lax.broadcasted_iota(jnp.int32, (slots, reach), 1) == face_cols[:, f : f + 1]
        )

    spread_mode = spread_mode_ref[...]
    spread_quant = spread_quant_ref[...]

    def expand(table, spread, transposed):
        hi, lo = halves(table)
        dims = ((1,), (1,)) if transposed else ((1,), (0,))
        left = dot(spread, hi, dims) + dot(spread, lo, dims)
        hi, lo = halves(left)
        return dot(hi, spread, nt) + dot(lo, spread, nt)

    def fill(ref, column, modes, quants):
        hi, lo = halves(modes * quants)
        at = slice(column * width, (column + 1) * width)
        ref[0:width, at] = hi
        ref[width : 2 * width, at] = hi
        ref[2 * width : 3 * width, at] = lo

    for c in range(dirs):
        quants = expand(star_ref[c], spread_quant, False)
        fill(w_derive, c, expand(stiff_ref[c], spread_mode, False), -quants)
        fill(w_local, c, expand(stiff_ref[c], spread_mode, True), quants)
    for f in range(faces):
        quants = expand(solver_minus_ref[f], spread_quant, False)
        fill(w_local, dirs + f, expand(face_minus_ref[f], spread_mode, True), -quants)
        quants = expand(solver_plus_ref[f], spread_quant, False)
        fill(w_plus.at[f], 0, expand(face_plus_ref[f], spread_mode, True), -quants)

    wait_all(send_a, recv_a, send_sem, recv_sem)
    for r in range(n):
        state[r * cap : (r + 1) * cap, :] = recv_a[r]

    start = state[...]
    scale = [start[:, extra_at + i : extra_at + i + 1] for i in range(dirs + faces)]
    weight = start[:, extra_at + dirs + faces : extra_at + dirs + faces + 1]
    occupied = (weight > 0.5).astype(jnp.float32)
    slow = (weight > 1.5).astype(jnp.float32)

    def derive(current):
        wide = dot(triple(current), w_derive[...])
        total = scale[0] * wide[:, 0:width]
        for c in range(1, dirs):
            total = total + scale[c] * wide[:, c * width : (c + 1) * width]
        return total

    def advance(values, current, step):
        hi, lo = halves(values)
        both = jnp.concatenate([hi, lo], axis=1)
        for b in range(beside):
            out = dot(pick_ghost[b].astype(jnp.bfloat16), both)
            ghost_send[step, b] = out[:, 0:width] + out[:, width:]
        copies = []
        for b, offset in enumerate(neighbour_steps):
            copy = pltpu.make_async_remote_copy(
                src_ref=ghost_send.at[step, b],
                dst_ref=ghost_recv.at[step, b],
                send_sem=ghost_send_sem.at[step, b],
                recv_sem=ghost_recv_sem.at[step, b],
                device_id=(lax.rem(me + offset + n, n),),
                device_id_type=MESH,
            )
            copy.start()
            copies.append(copy)
        wide = dot(jnp.concatenate([hi, lo, hi], axis=1), w_local[...])
        change = scale[0] * wide[:, 0:width]
        for i in range(1, dirs + faces):
            change = change + scale[i] * wide[:, i * width : (i + 1) * width]
        for copy in copies:
            copy.wait()
        arrived = jnp.concatenate([ghost_recv[step, b] for b in range(beside)], axis=0)
        ghost_hi, ghost_lo = halves(arrived)
        table = jnp.concatenate(
            [both, jnp.concatenate([ghost_hi, ghost_lo], axis=1)], axis=0
        )
        for f in range(faces):
            picked = dot(pick_face[f], table).astype(jnp.bfloat16)
            picked = jnp.concatenate([picked, picked[:, 0:width]], axis=1)
            change = change + scale[dirs + f] * dot(picked, w_plus[f])
        return current + occupied * change

    near, far = coefficients(0.0, 1.0), coefficients(1.0, 2.0)
    first = start * near[0]
    later = start * far[0]
    current = start
    for k in range(1, ORDER):
        current = derive(current)
        first = first + current * near[k]
        later = later + current * far[k]
    later_ref[...] = later
    middle = advance(first, start, 0)
    fresh = middle * near[0]
    current = middle
    for k in range(1, ORDER):
        current = derive(current)
        fresh = fresh + current * near[k]
    second = jnp.where(slow > 0.5, later_ref[...], fresh)
    final = advance(second, middle, 1)
    for r in range(n):
        send_b[r] = final[r * cap : (r + 1) * cap, :]
    start_all(send_b, recv_b, back_send_sem, back_recv_sem)
    wait_all(send_b, recv_b, back_send_sem, back_recv_sem)
    for r in range(n):
        state[r * cap : (r + 1) * cap, :] = recv_b[r]
    hi, mid, lo = thirds(state[...])
    back = pick_back[...]
    home = (dot(back, lo) + dot(back, mid)) + dot(back, hi)
    out_ref[...] = jnp.transpose(home)[0:flat, :]


def local(
    n,
    modal_dofs,
    jacobian,
    face_area,
    cluster_id,
    target_slot,
    ghost_slots,
    face_neighbours,
    stiffness,
    star_matrix,
    face_minus,
    face_plus,
    solver_minus,
    solver_plus,
):
    modes, quants, elements = modal_dofs.shape
    flat = modes * quants
    slots = face_neighbours.shape[1]
    faces, dirs = face_area.shape[0], jacobian.shape[0]
    cap = slots // n
    beside, ghosts = ghost_slots.shape[1:]
    extra_at = round_up(flat, SUB)
    width = round_up(extra_at + dirs + faces + 1, LANES)
    feature = np.arange(width)
    live = feature < flat
    spread_mode = (feature[:, None] // quants == np.arange(modes)[None, :]) & live[:, None]
    spread_quant = (feature[:, None] % quants == np.arange(quants)[None, :]) & live[:, None]
    vmem = pl.BlockSpec(memory_space=pltpu.VMEM)
    f32, bf16 = jnp.float32, jnp.bfloat16
    dma = pltpu.SemaphoreType.DMA
    args = (
        modal_dofs.reshape(flat, elements),
        jacobian,
        face_area,
        cluster_id.reshape(1, elements),
        target_slot.reshape(1, elements),
        ghost_slots.reshape(beside, ghosts),
        face_neighbours,
        jnp.asarray(spread_mode, bf16),
        jnp.asarray(spread_quant, bf16),
        stiffness,
        star_matrix,
        face_minus,
        face_plus,
        solver_minus,
        solver_plus,
    )
    out = pl.pallas_call(
        functools.partial(kernel, n, extra_at),
        out_shape=jax.ShapeDtypeStruct((flat, elements), f32),
        in_specs=[vmem] * len(args),
        out_specs=vmem,
        scratch_shapes=[
            pltpu.VMEM((width, elements), f32),
            pltpu.VMEM((n, cap, width), f32),
            pltpu.VMEM((n, cap, width), f32),
            pltpu.VMEM((n, cap, width), f32),
            pltpu.VMEM((n, cap, width), f32),
            pltpu.VMEM((2, beside, SUB, width), f32),
            pltpu.VMEM((2, beside, SUB, width), f32),
            pltpu.VMEM((slots, width), f32),
            pltpu.VMEM((slots, width), f32),
            pltpu.VMEM((3 * width, dirs * width), bf16),
            pltpu.VMEM((3 * width, (dirs + faces) * width), bf16),
            pltpu.VMEM((faces, 3 * width, width), bf16),
            pltpu.VMEM((faces, slots, slots + beside * SUB), bf16),
            pltpu.VMEM((beside, SUB, slots), f32),
            pltpu.VMEM((elements, slots), bf16),
            pltpu.VMEM((beside, LANES), f32),
            pltpu.VMEM((SUB, slots), f32),
            pltpu.VMEM((SUB, elements), f32),
            dma((n,)),
            dma((n,)),
            dma((n,)),
            dma((n,)),
            dma((2, beside)),
            dma((2, beside)),
        ],
        compiler_params=pltpu.CompilerParams(
            collective_id=0, has_side_effects=True, vmem_limit_bytes=56 * 2**20
        ),
    )(*args)
    return out.reshape(modes, quants, elements)


def solution(mesh):
    placed = (
        P(None, None, "dom"),
        P(None, "dom"),
        P(None, "dom"),
        P("dom"),
        P("dom"),
        P("dom", None, None),
        P(None, "dom"),
        P(),
        P(),
        P(),
        P(),
        P(),
        P(),
    )
    return jax.shard_map(
        functools.partial(local, mesh.shape["dom"]),
        mesh=mesh,
        in_specs=placed,
        out_specs=P(None, None, "dom"),
        check_vma=False,
    )
```

profile of v0, /device:TPU:15, one launch (start us, length us, event | category | flops | bytes accessed | tf_op | source)
XLA Modules:
  0.0 82.1 jit_solution(17921395187885080051)
XLA Ops:
  0.0 1.1 %copy.24 = f32[35,9,256]{2,1,0:T(8,128)S(1)} copy(f32[35,9,256]{2,0,1:T(8,128)} %param.15) | data formatting | bytes 645120 | tf_op args[0]
  1.1 0.0 copy-start
  1.1 0.8 reshape.15.dofs_ref
  1.9 0.1 copy-done
  2.0 0.0 copy-start.1
  2.0 0.6 copy.27.face_minus_ref
  2.6 0.3 copy-done.1
  2.9 0.0 copy-start.2
  2.9 0.6 copy.28.face_plus_ref
  3.5 0.1 copy-done.2
  3.6 0.0 copy-start.3
  3.6 0.6 copy.29.solver_minus_ref
  4.2 0.1 copy-done.3
  4.4 0.0 copy-start.4
  4.4 0.6 copy.30.solver_plus_ref
  5.0 0.1 copy-done.4
  5.1 0.0 copy-start.5
  5.1 0.6 copy.26.star_ref
  5.7 0.1 copy-done.5
  5.8 0.7 copy.25
  6.4 73.7 %shard_map.145 = f32[315,256]{1,0:T(8,128)} custom-call(f32[315,256]{1,0:T(8,128)} %reshape.15.dofs_ref, f32[3,256]{1,0:T(4,128)} %jac_ref.1, f32[4,256]{1,0:T(4,128)} %area_ref.1, s32[1,256]{1,0:T(1,128)} %bitcast.4, s32[1,256]{1,0:T(1,128)} %bitcast.5, s32[8,6]{1,0:T(8,128)} %bitcast.3, s32[4,384]{1,0:T(4,128)} %face_ref.1, ...), custom_call_target="tpu_custom_call" | custom-call | tf_op jit(solution)/shard_map/pallas_call | solution.py:346
  80.1 1.0 %reshape.19 = f32[35,9,256]{2,1,0:T(8,128)S(1)} reshape(f32[315,256]{1,0:T(8,128)} %shard_map.145) | data formatting | bytes 645120 | tf_op jit(solution)/shard_map/reshape | solution.py:381
  81.2 0.9 %copy.31 = f32[35,9,256]{2,0,1:T(8,128)} copy(f32[35,9,256]{2,1,0:T(8,128)S(1)} %reshape.19) | data formatting | bytes 645120 | tf_op jit(solution)/shard_map/reshape | solution.py:381
Async XLA Ops:
  1.1 0.9 %copy-start = (f32[4,35,35]{2,0,1:T(4,128)S(1)}, f32[4,35,35]{2,0,1:T(4,128)}, u32[]{:S(2)}) copy-start(f32[4,35,35]{2,0,1:T(4,128)} %param.24) | copy-start | bytes 58804
  2.0 0.9 %copy-start.1 = (f32[4,35,35]{2,0,1:T(4,128)S(1)}, f32[4,35,35]{2,0,1:T(4,128)}, u32[]{:S(2)}) copy-start(f32[4,35,35]{2,0,1:T(4,128)} %param.25) | copy-start | bytes 58804
  2.9 0.7 copy-start.2
  3.6 0.7 copy-start.3
  4.4 0.7 copy-start.4
  5.1 0.7 copy-start.5
where the time goes:
time: 82.6 us; the launch traced here: 82.1 us
  Pallas kernels  73.7 us (89%)
  local copies, waits for them, and re-layouts  8.36 us (10%)
    pallas_call x1, Pallas kernels, local(): pl.pallas_call(functools.partial(kernel, n, extra_at), out_shape=jax.Shap...  73.7 us
    unnamed x19, local copies, waits for them, and re-layouts  5.63 us
    reshape x2, local copies, waits for them, and re-layouts, local(): return out.reshape(modes, quants, elements)  1.95 us

commit v1 on v0

--- a/solution.py
+++ b/solution.py
@@ -99,12 +99,13 @@
     ghost_recv_sem,
 ):
     me = lax.axis_index("dom")
-    flat, elements = dofs_ref.shape
+    quants, modes, elements = dofs_ref.shape
+    pitch = extra_at // quants
     width = staged.shape[0]
     slots = state.shape[0]
     cap = slots // n
     beside = len(neighbour_steps)
-    ghosts = ghost_ref.shape[1]
+    ghosts = ghost_ref.shape[0]
     faces = face_ref.shape[0]
     dirs = stiff_ref.shape[0]
 
@@ -117,7 +118,8 @@
     lax.fori_loop(1, n, greet, 0)
 
     staged[...] = jnp.zeros_like(staged)
-    staged[0:flat, :] = dofs_ref[...]
+    for q in range(quants):
+        staged[q * pitch : q * pitch + modes, :] = dofs_ref[q]
     staged[extra_at : extra_at + dirs, :] = jac_ref[...]
     staged[extra_at + dirs : extra_at + dirs + faces, :] = area_ref[...]
     staged[extra_at + dirs + faces : extra_at + dirs + faces + 1, :] = 1.0 + cluster_ref[
@@ -168,9 +170,10 @@
     pick_back[...] = as_bf16(
         lax.broadcasted_iota(jnp.int32, (elements, slots), 1) == target_col
     )
-    ghost_idx[...] = jnp.full_like(ghost_idx, -1.0)
-    ghost_idx[:, 0:ghosts] = ghost_ref[...].astype(jnp.float32)
-    ghost_cols = jnp.transpose(ghost_idx[...])[0:SUB, :].astype(jnp.int32)
+    ghost_idx[...] = jnp.full_like(ghost_idx, -1)
+    for i in range(ghosts):
+        ghost_idx[i : i + 1, :] = ghost_ref[i]
+    ghost_cols = ghost_idx[...]
     place = lax.broadcasted_iota(jnp.int32, (SUB, slots), 1)
     for b in range(beside):
         pick_ghost[b] = (place == ghost_cols[:, b : b + 1]).astype(jnp.float32)
@@ -197,22 +200,22 @@
         hi, lo = halves(left)
         return dot(hi, spread, nt) + dot(lo, spread, nt)
 
-    def fill(ref, column, modes, quants):
-        hi, lo = halves(modes * quants)
+    def fill(ref, column, mode_part, quant_part):
+        hi, lo = halves(mode_part * quant_part)
         at = slice(column * width, (column + 1) * width)
         ref[0:width, at] = hi
         ref[width : 2 * width, at] = hi
         ref[2 * width : 3 * width, at] = lo
 
     for c in range(dirs):
-        quants = expand(star_ref[c], spread_quant, False)
-        fill(w_derive, c, expand(stiff_ref[c], spread_mode, False), -quants)
-        fill(w_local, c, expand(stiff_ref[c], spread_mode, True), quants)
+        solver = expand(star_ref[:, c, :], spread_quant, False)
+        fill(w_derive, c, expand(stiff_ref[c], spread_mode, False), -solver)
+        fill(w_local, c, expand(stiff_ref[c], spread_mode, True), solver)
     for f in range(faces):
-        quants = expand(solver_minus_ref[f], spread_quant, False)
-        fill(w_local, dirs + f, expand(face_minus_ref[f], spread_mode, True), -quants)
-        quants = expand(solver_plus_ref[f], spread_quant, False)
-        fill(w_plus.at[f], 0, expand(face_plus_ref[f], spread_mode, True), -quants)
+        solver = expand(solver_minus_ref[:, f, :], spread_quant, False)
+        fill(w_local, dirs + f, expand(face_minus_ref[:, f, :], spread_mode, True), -solver)
+        solver = expand(solver_plus_ref[:, f, :], spread_quant, False)
+        fill(w_plus.at[f], 0, expand(face_plus_ref[:, f, :], spread_mode, True), -solver)
 
     wait_all(send_a, recv_a, send_sem, recv_sem)
     for r in range(n):
@@ -292,7 +295,9 @@
     hi, mid, lo = thirds(state[...])
     back = pick_back[...]
     home = (dot(back, lo) + dot(back, mid)) + dot(back, hi)
-    out_ref[...] = jnp.transpose(home)[0:flat, :]
+    home = jnp.transpose(home)
+    for q in range(quants):
+        out_ref[q] = home[q * pitch : q * pitch + modes, :]
 
 
 def local(
@@ -312,40 +317,40 @@
     solver_plus,
 ):
     modes, quants, elements = modal_dofs.shape
-    flat = modes * quants
+    pitch = round_up(modes, SUB)
     slots = face_neighbours.shape[1]
     faces, dirs = face_area.shape[0], jacobian.shape[0]
     cap = slots // n
     beside, ghosts = ghost_slots.shape[1:]
-    extra_at = round_up(flat, SUB)
+    extra_at = quants * pitch
     width = round_up(extra_at + dirs + faces + 1, LANES)
     feature = np.arange(width)
-    live = feature < flat
-    spread_mode = (feature[:, None] // quants == np.arange(modes)[None, :]) & live[:, None]
-    spread_quant = (feature[:, None] % quants == np.arange(quants)[None, :]) & live[:, None]
+    live = (feature < extra_at) & (feature % pitch < modes)
+    spread_mode = (feature[:, None] % pitch == np.arange(modes)[None, :]) & live[:, None]
+    spread_quant = (feature[:, None] // pitch == np.arange(quants)[None, :]) & live[:, None]
     vmem = pl.BlockSpec(memory_space=pltpu.VMEM)
     f32, bf16 = jnp.float32, jnp.bfloat16
     dma = pltpu.SemaphoreType.DMA
     args = (
-        modal_dofs.reshape(flat, elements),
+        jnp.transpose(modal_dofs, (1, 0, 2)),
         jacobian,
         face_area,
         cluster_id.reshape(1, elements),
         target_slot.reshape(1, elements),
-        ghost_slots.reshape(beside, ghosts),
+        jnp.transpose(ghost_slots, (2, 0, 1)),
         face_neighbours,
         jnp.asarray(spread_mode, bf16),
         jnp.asarray(spread_quant, bf16),
         stiffness,
-        star_matrix,
-        face_minus,
-        face_plus,
-        solver_minus,
-        solver_plus,
+        jnp.transpose(star_matrix, (1, 0, 2)),
+        jnp.transpose(face_minus, (1, 0, 2)),
+        jnp.transpose(face_plus, (1, 0, 2)),
+        jnp.transpose(solver_minus, (1, 0, 2)),
+        jnp.transpose(solver_plus, (1, 0, 2)),
     )
     out = pl.pallas_call(
         functools.partial(kernel, n, extra_at),
-        out_shape=jax.ShapeDtypeStruct((flat, elements), f32),
+        out_shape=jax.ShapeDtypeStruct((quants, modes, elements), f32),
         in_specs=[vmem] * len(args),
         out_specs=vmem,
         scratch_shapes=[
@@ -364,7 +369,7 @@
             pltpu.VMEM((faces, slots, slots + beside * SUB), bf16),
             pltpu.VMEM((beside, SUB, slots), f32),
             pltpu.VMEM((elements, slots), bf16),
-            pltpu.VMEM((beside, LANES), f32),
+            pltpu.VMEM((SUB, beside), jnp.int32),
             pltpu.VMEM((SUB, slots), f32),
             pltpu.VMEM((SUB, elements), f32),
             dma((n,)),
@@ -378,7 +383,7 @@
             collective_id=0, has_side_effects=True, vmem_limit_bytes=56 * 2**20
         ),
     )(*args)
-    return out.reshape(modes, quants, elements)
+    return jnp.transpose(out, (1, 0, 2))
 
 
 def solution(mesh):

time: 82.6 us -> 75.7 us (0.916)
  local copies, waits for them, and re-layouts: 8.36 us -> 1.75 us
    unnamed x19 -> x1, local copies, waits for them, and re-layouts: 5.63 us -> 1.75 us
    reshape x3 -> x0, local copies, waits for them, and re-layouts: 2.73 us -> none  [the longest x2 1.95 us: local(): return out.reshape(modes, quants, elements)]
where the time goes in v1:
time: 75.7 us; the launch traced here: 75.5 us
  Pallas kernels  73.7 us (97%)
  local copies, waits for them, and re-layouts  1.75 us (2%)
    pallas_call x1, Pallas kernels, local(): pl.pallas_call(functools.partial(kernel, n, extra_at), out_shape=jax.Shap...  73.7 us
    unnamed x1, local copies, waits for them, and re-layouts  1.75 us

profile of v1, /device:TPU:15, one launch (start us, length us, event | category | flops | bytes accessed | tf_op | source)
XLA Modules:
  0.0 75.5 jit_solution(1229512450807278944)
XLA Ops:
  0.0 73.7 %shard_map.145 = f32[9,35,256]{2,1,0:T(8,128)} custom-call(f32[9,35,256]{2,1,0:T(8,128)} %bitcast.11, f32[3,256]{1,0:T(4,128)} %jac_ref.1, f32[4,256]{1,0:T(4,128)} %area_ref.1, s32[1,256]{1,0:T(1,128)} %bitcast.18, s32[1,256]{1,0:T(1,128)} %bitcast.19, s32[6,1,8]{2,1,0:T(1,128)} %bitcast.17, s32[4,384]{1,0:T(4,128)} %face_ref.1, ...), custom_call_target="tpu_custom_call" | custom-call | tf_op jit(solution)/shard_map/pallas_call | solution.py:351
  73.7 1.7 %copy.17 = f32[35,9,256]{2,0,1:T(8,128)} copy(f32[35,9,256]{2,0,1:T(8,128)} %bitcast.10) | data formatting | bytes 645120

commit v2 on v1

--- a/solution.py
+++ b/solution.py
@@ -56,7 +56,6 @@
 
 def kernel(
     n,
-    extra_at,
     dofs_ref,
     jac_ref,
     area_ref,
@@ -81,6 +80,8 @@
     ghost_send,
     ghost_recv,
     state,
+    extra_rows,
+    first_ref,
     later_ref,
     w_derive,
     w_local,
@@ -91,6 +92,7 @@
     ghost_idx,
     face_idx,
     target_idx,
+    extras,
     send_sem,
     recv_sem,
     back_send_sem,
@@ -100,10 +102,17 @@
 ):
     me = lax.axis_index("dom")
     quants, modes, elements = dofs_ref.shape
-    pitch = extra_at // quants
-    width = staged.shape[0]
+    flat = quants * modes
+    width = state.shape[1]
+    whole_tiles = width // LANES - 1
     slots = state.shape[0]
     cap = slots // n
+    paired = -(-cap // 2)
+    half = n // 2
+    half_rows = half * cap
+    near_base = half * (me // half)
+    far_base = half - near_base
+    turn = far_base * cap
     beside = len(neighbour_steps)
     ghosts = ghost_ref.shape[0]
     faces = face_ref.shape[0]
@@ -117,56 +126,124 @@
 
     lax.fori_loop(1, n, greet, 0)
 
+    def row_of(slot):
+        moved = slot - turn
+        return moved + slots * (moved < 0).astype(jnp.int32)
+
+    own_lanes = lax.broadcasted_iota(jnp.int32, (cap, LANES), 0) == (
+        lax.broadcasted_iota(jnp.int32, (cap, LANES), 1) // SUB
+    )
+
+    def pack(values, buffer, owners):
+        side = values[:, whole_tiles * LANES : width]
+        turned = pltpu.roll(side, LANES // 2, 1)
+        for j, owner in enumerate(owners):
+            lo = j * cap
+            for t in range(whole_tiles):
+                buffer[owner, t * cap : (t + 1) * cap, :] = values[
+                    lo : lo + cap, t * LANES : (t + 1) * LANES
+                ]
+            at = whole_tiles * cap
+            upper = cap - paired
+            if upper < paired:
+                buffer[owner, at : at + paired, :] = side[lo : lo + paired]
+            buffer[owner, at : at + upper, :] = (
+                side[lo : lo + upper] + turned[lo + paired : lo + cap]
+            )
+
+    def unpack(buffer, part):
+        first_owner = far_base if part == 0 else near_base
+        for j in range(half):
+            owner = first_owner + j
+            lo = part * half_rows + j * cap
+            for t in range(whole_tiles):
+                state[lo : lo + cap, t * LANES : (t + 1) * LANES] = buffer[
+                    owner, t * cap : (t + 1) * cap, :
+                ]
+            at = whole_tiles * cap
+            side = buffer[owner, at : at + paired, :]
+            turned = pltpu.roll(side, LANES // 2, 1)
+            state[lo : lo + paired, whole_tiles * LANES : width] = side
+            state[lo + paired : lo + cap, whole_tiles * LANES : width] = turned[0 : cap - paired]
+        values = state[part * half_rows : (part + 1) * half_rows, :]
+        lane = lax.broadcasted_iota(jnp.int32, values.shape, 1)
+        return jnp.where(lane < flat, values, 0.0)
+
     staged[...] = jnp.zeros_like(staged)
     for q in range(quants):
-        staged[q * pitch : q * pitch + modes, :] = dofs_ref[q]
-    staged[extra_at : extra_at + dirs, :] = jac_ref[...]
-    staged[extra_at + dirs : extra_at + dirs + faces, :] = area_ref[...]
-    staged[extra_at + dirs + faces : extra_at + dirs + faces + 1, :] = 1.0 + cluster_ref[
-        ...
-    ].astype(jnp.float32)
+        staged[q * modes : (q + 1) * modes, :] = dofs_ref[q]
+    extras[...] = jnp.zeros_like(extras)
+    extras[0:dirs, :] = jac_ref[...]
+    extras[dirs : dirs + faces, :] = area_ref[...]
+    extras[dirs + faces : dirs + faces + 1, :] = 1.0 + cluster_ref[...].astype(jnp.float32)
+    staged[width : width + LANES, :] = jnp.concatenate([extras[...]] * (LANES // SUB), axis=0)
     scatter = as_bf16(
         lax.broadcasted_iota(jnp.int32, (slots, elements), 0) == target_ref[...]
     )
     hi, mid, lo = thirds(staged[...])
     nt = ((1,), (1,))
     rows = (dot(scatter, lo, nt) + dot(scatter, mid, nt)) + dot(scatter, hi, nt)
-    for r in range(n):
-        send_a[r] = rows[r * cap : (r + 1) * cap, :]
+    pack(rows[:, 0:width], send_a, range(n))
+    extra_row = whole_tiles * cap + paired
+    for o in range(n):
+        listed = jnp.where(own_lanes, rows[o * cap : (o + 1) * cap, width : width + LANES], 0.0)
+        send_a[o, extra_row : extra_row + 1, :] = jnp.sum(listed, axis=0, keepdims=True)
 
     pl.semaphore_wait(barrier, n - 1)
 
-    def piece(source, landing, out_sem, in_sem, d):
-        peer = lax.rem(me + d, n)
+    def outgoing(source, landing, out_sem, in_sem, peer):
         return pltpu.make_async_remote_copy(
             src_ref=source.at[peer],
             dst_ref=landing.at[me],
-            send_sem=out_sem.at[d],
-            recv_sem=in_sem.at[d],
+            send_sem=out_sem.at[peer],
+            recv_sem=in_sem.at[me],
             device_id=(peer,),
             device_id_type=MESH,
         )
 
-    def start_all(source, landing, out_sem, in_sem):
-        def body(d, carry):
-            piece(source, landing, out_sem, in_sem, d).start()
+    def incoming(source, landing, out_sem, in_sem, peer):
+        return pltpu.make_async_remote_copy(
+            src_ref=source.at[peer],
+            dst_ref=landing.at[peer],
+            send_sem=out_sem.at[peer],
+            recv_sem=in_sem.at[peer],
+            device_id=(peer,),
+            device_id_type=MESH,
+        )
+
+    mine = me - near_base
+
+    def far_peer(j):
+        return far_base + lax.rem(mine + j, half)
+
+    def near_peer(j):
+        return near_base + lax.rem(mine + j, half)
+
+    def each(peer_of, first, action, *refs):
+        def body(j, carry):
+            action(*refs, peer_of(j))
             return carry
 
-        lax.fori_loop(1, n, body, 0)
-        landing[me] = source[me]
-
-    def wait_all(source, landing, out_sem, in_sem):
-        def body(d, carry):
-            piece(source, landing, out_sem, in_sem, d).wait()
-            return carry
-
-        lax.fori_loop(1, n, body, 0)
-
-    start_all(send_a, recv_a, send_sem, recv_sem)
+        lax.fori_loop(first, half, body, 0)
+
+    def start(*refs):
+        outgoing(*refs).start()
+
+    def wait_in(*refs):
+        incoming(*refs).wait_recv()
+
+    def wait_out(*refs):
+        outgoing(*refs).wait_send()
+
+    forth = (send_a, recv_a, send_sem, recv_sem)
+    back = (send_b, recv_b, back_send_sem, back_recv_sem)
+    each(far_peer, 0, start, *forth)
+    each(near_peer, 1, start, *forth)
+    recv_a[me] = send_a[me]
 
     target_idx[...] = jnp.zeros_like(target_idx)
     target_idx[0:1, :] = target_ref[...].astype(jnp.float32)
-    target_col = jnp.transpose(target_idx[...])[:, 0:1].astype(jnp.int32)
+    target_col = row_of(jnp.transpose(target_idx[...])[:, 0:1].astype(jnp.int32))
     pick_back[...] = as_bf16(
         lax.broadcasted_iota(jnp.int32, (elements, slots), 1) == target_col
     )
@@ -174,6 +251,7 @@
     for i in range(ghosts):
         ghost_idx[i : i + 1, :] = ghost_ref[i]
     ghost_cols = ghost_idx[...]
+    ghost_cols = jnp.where(ghost_cols < 0, -1, row_of(ghost_cols))
     place = lax.broadcasted_iota(jnp.int32, (SUB, slots), 1)
     for b in range(beside):
         pick_ghost[b] = (place == ghost_cols[:, b : b + 1]).astype(jnp.float32)
@@ -182,8 +260,12 @@
     shift = jnp.zeros_like(listed)
     for b in range(1, beside):
         shift = shift + (listed >= slots + b * ghosts).astype(jnp.int32) * (SUB - ghosts)
-    face_idx[0:faces, :] = (listed + shift).astype(jnp.float32)
-    face_cols = jnp.transpose(face_idx[...]).astype(jnp.int32)
+    listed = jnp.where(listed < slots, row_of(listed), listed + shift)
+    face_idx[0:faces, :] = listed.astype(jnp.float32)
+    face_cols = jnp.transpose(face_idx[...])
+    flipped = jnp.concatenate([face_cols[half_rows:], face_cols[:half_rows]], axis=0)
+    moved = (jnp.zeros_like(face_cols) + turn) > 0.5
+    face_cols = jnp.where(moved, flipped, face_cols).astype(jnp.int32)
     reach = pick_face.shape[2]
     for f in range(faces):
         pick_face[f] = as_bf16(
@@ -217,30 +299,67 @@
         solver = expand(solver_plus_ref[:, f, :], spread_quant, False)
         fill(w_plus.at[f], 0, expand(face_plus_ref[:, f, :], spread_mode, True), -solver)
 
-    wait_all(send_a, recv_a, send_sem, recv_sem)
-    for r in range(n):
-        state[r * cap : (r + 1) * cap, :] = recv_a[r]
-
-    start = state[...]
-    scale = [start[:, extra_at + i : extra_at + i + 1] for i in range(dirs + faces)]
-    weight = start[:, extra_at + dirs + faces : extra_at + dirs + faces + 1]
-    occupied = (weight > 0.5).astype(jnp.float32)
-    slow = (weight > 1.5).astype(jnp.float32)
-
-    def derive(current):
+    near, far = coefficients(0.0, 1.0), coefficients(1.0, 2.0)
+    fold = as_bf16(
+        lax.broadcasted_iota(jnp.int32, (LANES, LANES), 0) % SUB
+        == lax.broadcasted_iota(jnp.int32, (LANES, LANES), 1)
+    )
+
+    def derive(current, scale):
         wide = dot(triple(current), w_derive[...])
         total = scale[0] * wide[:, 0:width]
         for c in range(1, dirs):
             total = total + scale[c] * wide[:, c * width : (c + 1) * width]
         return total
 
-    def advance(values, current, step):
+    def part_rows(part):
+        return slice(part * half_rows, (part + 1) * half_rows)
+
+    scales, occupied, slow, starts = [None] * 2, [None] * 2, [None] * 2, [None] * 2
+    recv_rows = recv_a.shape[1]
+    for part in (1, 0):
+        if part == 1:
+            each(near_peer, 1, wait_in, *forth)
+        else:
+            each(far_peer, 0, wait_in, *forth)
+        first_owner = far_base if part == 0 else near_base
+        for j in range(half):
+            row = recv_a[first_owner + j, recv_rows - 1 : recv_rows, :]
+            lo = part * half_rows + j * cap
+            extra_rows[lo : lo + cap, :] = jnp.where(
+                own_lanes, jnp.broadcast_to(row, (cap, LANES)), 0.0
+            )
+        hi, mid, lo = thirds(extra_rows[part_rows(part), :])
+        listed = (dot(lo, fold) + dot(mid, fold)) + dot(hi, fold)
+        scales[part] = [listed[:, i : i + 1] for i in range(dirs + faces)]
+        weight = listed[:, dirs + faces : dirs + faces + 1]
+        occupied[part] = (weight > 0.5).astype(jnp.float32)
+        slow[part] = (weight > 1.5).astype(jnp.float32)
+        current = unpack(recv_a, part)
+        state[part_rows(part), :] = current
+        first = current * near[0]
+        later = current * far[0]
+        for k in range(1, ORDER):
+            current = derive(current, scales[part])
+            first = first + current * near[k]
+            later = later + current * far[k]
+        first_ref[part_rows(part), :] = first
+        later_ref[part_rows(part), :] = later
+
+    def joined(parts):
+        return jnp.concatenate(parts, axis=0)
+
+    scale_all = [joined([scales[0][i], scales[1][i]]) for i in range(dirs + faces)]
+    occupied_all = joined(occupied)
+    slow_all = joined(slow)
+
+    def exchange(values, step):
         hi, lo = halves(values)
         both = jnp.concatenate([hi, lo], axis=1)
-        for b in range(beside):
+        copies = []
+        for b, offset in enumerate(neighbour_steps):
             out = dot(pick_ghost[b].astype(jnp.bfloat16), both)
             ghost_send[step, b] = out[:, 0:width] + out[:, width:]
-        copies = []
         for b, offset in enumerate(neighbour_steps):
             copy = pltpu.make_async_remote_copy(
                 src_ref=ghost_send.at[step, b],
@@ -252,52 +371,75 @@
             )
             copy.start()
             copies.append(copy)
-        wide = dot(jnp.concatenate([hi, lo, hi], axis=1), w_local[...])
+        return both, copies
+
+    def own_change(both, rows, scale):
+        mine_part = both[rows]
+        wide = dot(jnp.concatenate([mine_part, mine_part[:, 0:width]], axis=1), w_local[...])
         change = scale[0] * wide[:, 0:width]
         for i in range(1, dirs + faces):
             change = change + scale[i] * wide[:, i * width : (i + 1) * width]
+        picked = [
+            dot(pick_face[f, rows, 0:slots], both).astype(jnp.bfloat16) for f in range(faces)
+        ]
+        return change, picked
+
+    def ghost_table(copies, step):
         for copy in copies:
             copy.wait()
-        arrived = jnp.concatenate([ghost_recv[step, b] for b in range(beside)], axis=0)
-        ghost_hi, ghost_lo = halves(arrived)
-        table = jnp.concatenate(
-            [both, jnp.concatenate([ghost_hi, ghost_lo], axis=1)], axis=0
-        )
+        hi, lo = halves(jnp.concatenate([ghost_recv[step, b] for b in range(beside)], axis=0))
+        return jnp.concatenate([hi, lo], axis=1)
+
+    def face_change(change, picked, table, rows, scale):
         for f in range(faces):
-            picked = dot(pick_face[f], table).astype(jnp.bfloat16)
-            picked = jnp.concatenate([picked, picked[:, 0:width]], axis=1)
-            change = change + scale[dirs + f] * dot(picked, w_plus[f])
-        return current + occupied * change
-
-    near, far = coefficients(0.0, 1.0), coefficients(1.0, 2.0)
-    first = start * near[0]
-    later = start * far[0]
-    current = start
-    for k in range(1, ORDER):
-        current = derive(current)
-        first = first + current * near[k]
-        later = later + current * far[k]
-    later_ref[...] = later
-    middle = advance(first, start, 0)
+            both = picked[f] + dot(pick_face[f, rows, slots:reach], table).astype(jnp.bfloat16)
+            both = jnp.concatenate([both, both[:, 0:width]], axis=1)
+            change = change + scale[dirs + f] * dot(both, w_plus[f])
+        return change
+
+    every = slice(0, slots)
+    both, copies = exchange(first_ref[...], 0)
+    change, picked = own_change(both, every, scale_all)
+    change = face_change(change, picked, ghost_table(copies, 0), every, scale_all)
+    middle = state[...] + occupied_all * change
+    state[...] = middle
     fresh = middle * near[0]
     current = middle
     for k in range(1, ORDER):
-        current = derive(current)
+        current = derive(current, scale_all)
         fresh = fresh + current * near[k]
-    second = jnp.where(slow > 0.5, later_ref[...], fresh)
-    final = advance(second, middle, 1)
-    for r in range(n):
-        send_b[r] = final[r * cap : (r + 1) * cap, :]
-    start_all(send_b, recv_b, back_send_sem, back_recv_sem)
-    wait_all(send_b, recv_b, back_send_sem, back_recv_sem)
-    for r in range(n):
-        state[r * cap : (r + 1) * cap, :] = recv_b[r]
-    hi, mid, lo = thirds(state[...])
-    back = pick_back[...]
-    home = (dot(back, lo) + dot(back, mid)) + dot(back, hi)
+    second = jnp.where(slow_all > 0.5, later_ref[...], fresh)
+    both, copies = exchange(second, 1)
+    for part in (0, 1):
+        rows = part_rows(part)
+        change, picked = own_change(both, rows, scales[part])
+        if part == 0:
+            table = ghost_table(copies, 1)
+        change = face_change(change, picked, table, rows, scales[part])
+        final = state[rows, :] + occupied[part] * change
+        first_owner = far_base if part == 0 else near_base
+        pack(final, send_b, [first_owner + j for j in range(half)])
+        if part == 0:
+            each(far_peer, 0, start, *back)
+        else:
+            each(near_peer, 1, start, *back)
+    recv_b[me] = send_b[me]
+    home = None
+    for part in (1, 0):
+        if part == 1:
+            each(near_peer, 1, wait_in, *back)
+        else:
+            each(far_peer, 0, wait_in, *back)
+        hi, mid, lo = thirds(unpack(recv_b, part))
+        table = pick_back[:, part_rows(part)]
+        piece = (dot(table, lo) + dot(table, mid)) + dot(table, hi)
+        home = piece if home is None else home + piece
     home = jnp.transpose(home)
     for q in range(quants):
-        out_ref[q] = home[q * pitch : q * pitch + modes, :]
+        out_ref[q] = home[q * modes : (q + 1) * modes, :]
+    for refs in (forth, back):
+        each(far_peer, 0, wait_out, *refs)
+        each(near_peer, 1, wait_out, *refs)
 
 
 def local(
@@ -317,17 +459,18 @@
     solver_plus,
 ):
     modes, quants, elements = modal_dofs.shape
-    pitch = round_up(modes, SUB)
+    flat = quants * modes
     slots = face_neighbours.shape[1]
     faces, dirs = face_area.shape[0], jacobian.shape[0]
     cap = slots // n
     beside, ghosts = ghost_slots.shape[1:]
-    extra_at = quants * pitch
-    width = round_up(extra_at + dirs + faces + 1, LANES)
+    width = round_up(flat, LANES)
+    wire_rows = (width // LANES - 1) * cap + -(-cap // 2)
+    assert width - flat >= LANES // 2 and cap * SUB <= LANES
     feature = np.arange(width)
-    live = (feature < extra_at) & (feature % pitch < modes)
-    spread_mode = (feature[:, None] % pitch == np.arange(modes)[None, :]) & live[:, None]
-    spread_quant = (feature[:, None] // pitch == np.arange(quants)[None, :]) & live[:, None]
+    live = feature < flat
+    spread_mode = (feature[:, None] % modes == np.arange(modes)[None, :]) & live[:, None]
+    spread_quant = (feature[:, None] // modes == np.arange(quants)[None, :]) & live[:, None]
     vmem = pl.BlockSpec(memory_space=pltpu.VMEM)
     f32, bf16 = jnp.float32, jnp.bfloat16
     dma = pltpu.SemaphoreType.DMA
@@ -349,18 +492,20 @@
         jnp.transpose(solver_plus, (1, 0, 2)),
     )
     out = pl.pallas_call(
-        functools.partial(kernel, n, extra_at),
+        functools.partial(kernel, n),
         out_shape=jax.ShapeDtypeStruct((quants, modes, elements), f32),
         in_specs=[vmem] * len(args),
         out_specs=vmem,
         scratch_shapes=[
-            pltpu.VMEM((width, elements), f32),
-            pltpu.VMEM((n, cap, width), f32),
-            pltpu.VMEM((n, cap, width), f32),
-            pltpu.VMEM((n, cap, width), f32),
-            pltpu.VMEM((n, cap, width), f32),
+            pltpu.VMEM((width + LANES, elements), f32),
+            pltpu.VMEM((n, wire_rows + 1, LANES), f32),
+            pltpu.VMEM((n, wire_rows + 1, LANES), f32),
+            pltpu.VMEM((n, wire_rows, LANES), f32),
+            pltpu.VMEM((n, wire_rows, LANES), f32),
             pltpu.VMEM((2, beside, SUB, width), f32),
             pltpu.VMEM((2, beside, SUB, width), f32),
+            pltpu.VMEM((slots, width), f32),
+            pltpu.VMEM((slots, LANES), f32),
             pltpu.VMEM((slots, width), f32),
             pltpu.VMEM((slots, width), f32),
             pltpu.VMEM((3 * width, dirs * width), bf16),
@@ -371,6 +516,7 @@
             pltpu.VMEM((elements, slots), bf16),
             pltpu.VMEM((SUB, beside), jnp.int32),
             pltpu.VMEM((SUB, slots), f32),
+            pltpu.VMEM((SUB, elements), f32),
             pltpu.VMEM((SUB, elements), f32),
             dma((n,)),
             dma((n,)),

time: 75.7 us -> 63.1 us (0.83)
  the two profiles are of different devices: /device:TPU:15 before, /device:TPU:0 now
where the time goes in v2:
time: 63.1 us; the launch traced here: 62.9 us
  Pallas kernels  61.1 us (97%)
  local copies, waits for them, and re-layouts  1.75 us (3%)
    pallas_call x1, Pallas kernels, local(): pl.pallas_call(functools.partial(kernel, n), out_shape=jax.ShapeDtypeStru...  61.1 us
    unnamed x1, local copies, waits for them, and re-layouts  1.75 us

profile of v2, /device:TPU:0, one launch (start us, length us, event | category | flops | bytes accessed | tf_op | source)
XLA Modules:
  0.0 62.9 jit_solution(13008463587066465220)
XLA Ops:
  0.0 61.1 %shard_map.145 = f32[9,35,256]{2,1,0:T(8,128)} custom-call(f32[9,35,256]{2,1,0:T(8,128)} %bitcast.11, f32[3,256]{1,0:T(4,128)} %jac_ref.1, f32[4,256]{1,0:T(4,128)} %area_ref.1, s32[1,256]{1,0:T(1,128)} %bitcast.18, s32[1,256]{1,0:T(1,128)} %bitcast.19, s32[6,1,8]{2,1,0:T(1,128)} %bitcast.17, s32[4,384]{1,0:T(4,128)} %face_ref.1, ...), custom_call_target="tpu_custom_call" | custom-call | tf_op jit(solution)/shard_map/pallas_call | solution.py:494
  61.2 1.7 %copy.17 = f32[35,9,256]{2,0,1:T(8,128)} copy(f32[35,9,256]{2,0,1:T(8,128)} %bitcast.10) | data formatting | bytes 645120
